TPU v7x, 32 devices: a whole 2x2x4 slice. The times are simulated.
32 devices in a mesh: dp: 8 (over z, core), tensor: 4 (over y, x).
Axes of the slice: x: 2, y: 2, z: 4, core: 2. Of those that a mesh axis runs over, the one named last changes fastest.
Arguments:
- tokens: bfloat16 [32768, 1024], P(('dp', 'tensor')), may hold values from -6 to 6
- lengths: int32 [16], P('dp'), may hold values from 512 to 2048, as said below
- out_grad: bfloat16 [32768, 1024], P(('dp', 'tensor')), may hold values from -6 to 6
- ln1_gain: float32 [1024], replicated, may hold values from 0.5 to 1.5
- ln2_gain: float32 [1024], replicated, may hold values from 0.5 to 1.5
- onorm_gain: float32 [128], replicated, may hold values from 0.5 to 1.5
- a_log: float32 [8], replicated, may hold values from -6 to 0.5
- dt_bias: float32 [8], replicated, may hold values from -4 to 0
- w_query: bfloat16 [1024, 1024], P('dp', 'tensor'), may hold values from -0.1875 to 0.1875
- w_key: bfloat16 [1024, 2048], P('dp', 'tensor'), may hold values from -0.1875 to 0.1875
- w_value: bfloat16 [1024, 2048], P('dp', 'tensor'), may hold values from -0.1875 to 0.1875
- w_rates: bfloat16 [1024, 24], P('dp', 'tensor'), may hold values from -0.1875 to 0.1875
- w_outgate: bfloat16 [1024, 1024], P('dp', 'tensor'), may hold values from -0.1875 to 0.1875
- w_out: bfloat16 [1024, 1024], P('tensor', 'dp'), may hold values from -0.375 to 0.375
- w_gate: bfloat16 [1024, 2816], P('dp', 'tensor'), may hold values from -0.1875 to 0.1875
- w_up: bfloat16 [1024, 2816], P('dp', 'tensor'), may hold values from -0.1875 to 0.1875
- w_down: bfloat16 [2816, 1024], P('tensor', 'dp'), may hold values from -0.21875 to 0.21875
Outputs:
- block_out: bfloat16 [32768, 1024], P(('dp', 'tensor'))
- tokens_grad: bfloat16 [32768, 1024], P(('dp', 'tensor'))
- ln1_gain_grad: float32 [1024], replicated
- ln2_gain_grad: float32 [1024], replicated
- onorm_gain_grad: float32 [128], replicated
- a_log_grad: float32 [8], replicated
- dt_bias_grad: float32 [8], replicated
- w_query_grad: float32 [1024, 1024], P('dp', 'tensor')
- w_key_grad: float32 [1024, 2048], P('dp', 'tensor')
- w_value_grad: float32 [1024, 2048], P('dp', 'tensor')
- w_rates_grad: float32 [1024, 24], P('dp', 'tensor')
- w_outgate_grad: float32 [1024, 1024], P('dp', 'tensor')
- w_out_grad: float32 [1024, 1024], P('tensor', 'dp')
- w_gate_grad: float32 [1024, 2816], P('dp', 'tensor')
- w_up_grad: float32 [1024, 2816], P('dp', 'tensor')
- w_down_grad: float32 [2816, 1024], P('tensor', 'dp')
Inputs may be any that keep to these rules, and one draw needn't show every extreme that they name: `lengths`: valid positions of each sequence; the positions after them are padding; in every draw some sequence has all 2048 positions valid.
All inputs are finite; a program needn't handle non-finite values.
Results may differ from a plain program's by a relative error of at most 0.017.
Values may be sent and summed in bfloat16 or wider, within the bound.
No kernel may reach another device: no remote copies, remote signals or barrier semaphores. Data moves between devices by JAX's collectives and lax.ppermute only.
A program may use at most 448 MiB of HBM per device.

v0:
```python
from functools import partial
import jax
import jax.numpy as jnp
from jax import lax
from jax.sharding import PartitionSpec as P

HEAD = 128
NH = 2
CT = 64
LEN = 2048
HIGH = lax.Precision.HIGHEST
EPS = 1e-06


def project(left, right):
    return jnp.dot(left, right, preferred_element_type=jnp.float32)


def times_trans(left, right):
    return lax.dot_general(
        left, right, (((1,), (1,)), ((), ())), preferred_element_type=jnp.float32
    )


def trans_times(left, right):
    return lax.dot_general(
        left, right, (((0,), (0,)), ((), ())), preferred_element_type=jnp.float32
    )


def rms_parts(values):
    scale = lax.rsqrt(jnp.mean(values * values, axis=-1, keepdims=True) + EPS)
    return (values * scale, scale)


def rms_back(grad_out, values, scale, gain):
    gain_grad = jnp.sum(grad_out * values * scale, axis=0)
    scaled = grad_out * gain
    value_grad = scale * scaled - values * scale * scale * scale * jnp.mean(
        scaled * values, axis=-1, keepdims=True
    )
    return (value_grad, gain_grad)


def unit_rows(values):
    return values * lax.rsqrt(jnp.sum(values * values, axis=-1, keepdims=True) + EPS)


def stretch_mixer(query, keys, values, betas, decays):
    batch, length, heads, width = query.shape
    steps = keys.shape[3]
    vwidth = values.shape[-1]
    span = CT * steps
    nblock = length // CT

    def blocked(array):
        moved = array.reshape((batch, nblock, CT, heads) + array.shape[3:])
        return jnp.moveaxis(jnp.moveaxis(moved, 1, 0), 3, 2)

    queries = blocked(query)
    key_rows = blocked(keys).reshape(nblock, batch, heads, span, width)
    value_rows = blocked(values).reshape(nblock, batch, heads, span, vwidth)
    beta_rows = blocked(betas).reshape(nblock, batch, heads, span)
    log_decay = jnp.concatenate(
        [decays[..., None], jnp.zeros(decays.shape + (steps - 1,), jnp.float32)], axis=-1
    )
    cumul = jnp.cumsum(blocked(log_decay).reshape(nblock, batch, heads, span), axis=-1)
    index = jnp.arange(span)
    strict = index[:, None] > index[None, :]
    apart = cumul[..., :, None] - cumul[..., None, :]
    weights_strict = jnp.where(strict, jnp.exp(jnp.minimum(apart, 0.0)), 0.0)
    intersections = jnp.einsum("nbhid,nbhjd->nbhij", key_rows, key_rows, precision=HIGH)
    lower = (
        jnp.eye(span, dtype=jnp.float32) + weights_strict * intersections * beta_rows[..., None, :]
    )
    growth = jnp.exp(cumul)
    solved = jax.scipy.linalg.solve_triangular(
        lower,
        jnp.concatenate([value_rows, growth[..., None] * key_rows], axis=-1),
        lower=True,
        unit_diagonal=True,
    )
    new_values = solved[..., :vwidth]
    key_mix = solved[..., vwidth:]
    read_at = jnp.arange(CT) * steps + steps - 1
    read_cumul = cumul.reshape(nblock, batch, heads, CT, steps)[..., steps - 1]
    read_apart = read_cumul[..., :, None] - cumul[..., None, :]
    upto = read_at[:, None] >= index[None, :]
    read_weights = jnp.where(upto, jnp.exp(jnp.minimum(read_apart, 0.0)), 0.0)
    scores = (
        jnp.einsum("nbhid,nbhjd->nbhij", queries, key_rows, precision=HIGH)
        * read_weights
        * beta_rows[..., None, :]
    )
    query_decayed = jnp.exp(read_cumul)[..., None] * queries
    tail = cumul[..., span - 1]
    key_out = (jnp.exp(tail[..., None] - cumul) * beta_rows)[..., None] * key_rows

    def advance(carried, block_in):
        new_v, mix_k, score, query_d, key_o, tail_b = block_in
        delta = new_v - jnp.einsum("bhpk,bhkv->bhpv", mix_k, carried, precision=HIGH)
        output = jnp.einsum("bhck,bhkv->bhcv", query_d, carried, precision=HIGH) + jnp.einsum(
            "bhcp,bhpv->bhcv", score, delta, precision=HIGH
        )
        carried = jnp.exp(tail_b)[..., None, None] * carried + jnp.einsum(
            "bhpk,bhpv->bhkv", key_o, delta, precision=HIGH
        )
        return (carried, output)

    initial = jnp.zeros((batch, heads, width, vwidth), jnp.float32)
    last_state, outputs = lax.scan(
        advance, initial, (new_values, key_mix, scores, query_decayed, key_out, tail)
    )
    outputs = jnp.moveaxis(jnp.moveaxis(outputs, 2, 3), 0, 1)
    return outputs.reshape(batch, length, heads, vwidth)


def mixer(query_pre, key_pre, value_pre, rates_pre, outgate_pre, a_here, dt_here, gain, seq_count):
    rows = query_pre.shape[0]
    lead_dims = (seq_count, rows // seq_count)
    heads = a_here.shape[0]
    query = unit_rows(jax.nn.silu(query_pre).reshape(lead_dims + (heads, HEAD)))
    keys = unit_rows(jax.nn.silu(key_pre).reshape(lead_dims + (heads, NH, HEAD)))
    values = jax.nn.silu(value_pre).reshape(lead_dims + (heads, NH, HEAD))
    rates = rates_pre.reshape(lead_dims + (heads, NH + 1))
    betas = jax.nn.sigmoid(rates[..., :NH])
    decays = -jnp.exp(a_here) * jax.nn.softplus(rates[..., NH] + dt_here)
    mixed = stretch_mixer(query, keys, values, betas, decays)
    gate = jax.nn.silu(outgate_pre.reshape(lead_dims + (heads, HEAD)))
    normed = mixed * lax.rsqrt(jnp.mean(mixed * mixed, axis=-1, keepdims=True) + EPS) * gain * gate
    return normed.reshape(rows, heads * HEAD)


def per_device(
    tokens,
    lengths,
    out_grad,
    ln1_gain,
    ln2_gain,
    onorm_gain,
    a_log,
    dt_bias,
    w_query,
    w_key,
    w_value,
    w_rates,
    w_outgate,
    w_out,
    w_gate,
    w_up,
    w_down,
):
    tensor_count = lax.axis_size("tensor")
    tensor_pos = lax.axis_index("tensor")
    tok_dev = tokens.shape[0]
    seq_count = lengths.shape[0]
    heads_here = a_log.shape[0] // tensor_count
    positions = tensor_pos * tok_dev + jnp.arange(tok_dev)
    owners = positions // LEN
    limits = jnp.sum(
        jnp.where(owners[:, None] == jnp.arange(seq_count)[None, :], lengths[None, :], 0), axis=1
    )
    mask = (positions % LEN < limits).astype(jnp.float32)[:, None]
    full_query, full_key, full_value, full_rates, full_outgate, full_out = (
        lax.all_gather(w_query, "dp", axis=0, tiled=True),
        lax.all_gather(w_key, "dp", axis=0, tiled=True),
        lax.all_gather(w_value, "dp", axis=0, tiled=True),
        lax.all_gather(w_rates, "dp", axis=0, tiled=True),
        lax.all_gather(w_outgate, "dp", axis=0, tiled=True),
        lax.all_gather(w_out, "dp", axis=1, tiled=True),
    )
    resid_in = tokens.astype(jnp.float32)
    normed_one, scale_one = rms_parts(resid_in)
    first_all = lax.all_gather(
        (normed_one * ln1_gain).astype(jnp.bfloat16), "tensor", axis=0, tiled=True
    )
    query_pre = project(first_all, full_query)
    key_pre = project(first_all, full_key)
    value_pre = project(first_all, full_value)
    rates_pre = project(first_all, full_rates)
    outgate_pre = project(first_all, full_outgate)
    a_here = lax.dynamic_slice_in_dim(a_log, tensor_pos * heads_here, heads_here)
    dt_here = lax.dynamic_slice_in_dim(dt_bias, tensor_pos * heads_here, heads_here)
    mixed, mixer_back = jax.vjp(
        partial(mixer, seq_count=seq_count),
        query_pre,
        key_pre,
        value_pre,
        rates_pre,
        outgate_pre,
        a_here,
        dt_here,
        onorm_gain,
    )
    mixed_low = mixed.astype(jnp.bfloat16)
    attn_sum = lax.psum_scatter(
        project(mixed_low, full_out), "tensor", scatter_dimension=0, tiled=True
    )
    middle = resid_in + attn_sum
    full_gate, full_up, full_down = (
        lax.all_gather(w_gate, "dp", axis=0, tiled=True),
        lax.all_gather(w_up, "dp", axis=0, tiled=True),
        lax.all_gather(w_down, "dp", axis=1, tiled=True),
    )
    normed_two, scale_two = rms_parts(middle)
    second_all = lax.all_gather(
        (normed_two * ln2_gain).astype(jnp.bfloat16), "tensor", axis=0, tiled=True
    )
    gate_pre = project(second_all, full_gate)
    up_pre = project(second_all, full_up)
    gate_sig = jax.nn.sigmoid(gate_pre)
    gate_act = gate_pre * gate_sig
    hidden = (gate_act * up_pre).astype(jnp.bfloat16)
    mlp_sum = lax.psum_scatter(
        project(hidden, full_down).astype(jnp.bfloat16), "tensor", scatter_dimension=0, tiled=True
    ).astype(jnp.float32)
    block_out = ((middle + mlp_sum) * mask).astype(jnp.bfloat16)
    grad_top = out_grad.astype(jnp.float32) * mask
    grad_all = lax.all_gather(grad_top.astype(jnp.bfloat16), "tensor", axis=0, tiled=True)
    hidden_grad = times_trans(grad_all, full_down)
    down_grad = trans_times(hidden, grad_all)
    up_grad_pre = (hidden_grad * gate_act).astype(jnp.bfloat16)
    gate_grad_pre = (hidden_grad * up_pre * gate_sig * (1.0 + gate_pre * (1.0 - gate_sig))).astype(
        jnp.bfloat16
    )
    gate_grad = trans_times(second_all, gate_grad_pre)
    up_grad = trans_times(second_all, up_grad_pre)
    second_grad = lax.psum_scatter(
        times_trans(gate_grad_pre, full_gate) + times_trans(up_grad_pre, full_up),
        "tensor",
        scatter_dimension=0,
        tiled=True,
    )
    middle_back, ln2_grad = rms_back(second_grad, middle, scale_two, ln2_gain)
    middle_grad = grad_top + middle_back
    middle_low = middle_grad.astype(jnp.bfloat16)
    middle_all = lax.all_gather(middle_low, "tensor", axis=0, tiled=True)
    out_proj_grad = trans_times(mixed_low, middle_all)
    mixed_grad = times_trans(middle_all, full_out)
    pulled = mixer_back(mixed_grad)
    pre_grads = tuple((item.astype(jnp.bfloat16) for item in pulled[:5]))
    weights_full = (full_query, full_key, full_value, full_rates, full_outgate)
    proj_grads = tuple((trans_times(first_all, item) for item in pre_grads))
    first_part = times_trans(pre_grads[0], weights_full[0])
    for which in range(1, 5):
        first_part = first_part + times_trans(pre_grads[which], weights_full[which])
    first_grad = lax.psum_scatter(
        first_part.astype(jnp.bfloat16), "tensor", scatter_dimension=0, tiled=True
    ).astype(jnp.float32)
    input_back, ln1_grad = rms_back(first_grad, resid_in, scale_one, ln1_gain)
    tokens_grad = (middle_grad + input_back).astype(jnp.bfloat16)
    a_grad = lax.dynamic_update_slice_in_dim(
        jnp.zeros_like(a_log), pulled[5], tensor_pos * heads_here, 0
    )
    dt_grad = lax.dynamic_update_slice_in_dim(
        jnp.zeros_like(dt_bias), pulled[6], tensor_pos * heads_here, 0
    )
    small = lax.psum((ln1_grad, ln2_grad, pulled[7], a_grad, dt_grad), ("dp", "tensor"))
    summed = (
        lax.psum_scatter(
            proj_grads[0].astype(jnp.bfloat16), "dp", scatter_dimension=0, tiled=True
        ).astype(jnp.float32),
        lax.psum_scatter(
            proj_grads[1].astype(jnp.bfloat16), "dp", scatter_dimension=0, tiled=True
        ).astype(jnp.float32),
        lax.psum_scatter(
            proj_grads[2].astype(jnp.bfloat16), "dp", scatter_dimension=0, tiled=True
        ).astype(jnp.float32),
        lax.psum_scatter(
            proj_grads[3].astype(jnp.bfloat16), "dp", scatter_dimension=0, tiled=True
        ).astype(jnp.float32),
        lax.psum_scatter(
            proj_grads[4].astype(jnp.bfloat16), "dp", scatter_dimension=0, tiled=True
        ).astype(jnp.float32),
        lax.psum_scatter(
            out_proj_grad.astype(jnp.bfloat16), "dp", scatter_dimension=1, tiled=True
        ).astype(jnp.float32),
        lax.psum_scatter(
            gate_grad.astype(jnp.bfloat16), "dp", scatter_dimension=0, tiled=True
        ).astype(jnp.float32),
        lax.psum_scatter(
            up_grad.astype(jnp.bfloat16), "dp", scatter_dimension=0, tiled=True
        ).astype(jnp.float32),
        lax.psum_scatter(
            down_grad.astype(jnp.bfloat16), "dp", scatter_dimension=1, tiled=True
        ).astype(jnp.float32),
    )
    return (
        block_out,
        tokens_grad,
        small[0],
        small[1],
        small[2],
        small[3],
        small[4],
        summed[0],
        summed[1],
        summed[2],
        summed[3],
        summed[4],
        summed[5],
        summed[6],
        summed[7],
        summed[8],
    )


def solution(mesh):
    in_specs = (
        P(("dp", "tensor"), None),
        P("dp"),
        P(("dp", "tensor"), None),
        P(),
        P(),
        P(),
        P(),
        P(),
        P("dp", "tensor"),
        P("dp", "tensor"),
        P("dp", "tensor"),
        P("dp", "tensor"),
        P("dp", "tensor"),
        P("tensor", "dp"),
        P("dp", "tensor"),
        P("dp", "tensor"),
        P("tensor", "dp"),
    )
    out_specs = (
        P(("dp", "tensor"), None),
        P(("dp", "tensor"), None),
        P(),
        P(),
        P(),
        P(),
        P(),
        P("dp", "tensor"),
        P("dp", "tensor"),
        P("dp", "tensor"),
        P("dp", "tensor"),
        P("dp", "tensor"),
        P("tensor", "dp"),
        P("dp", "tensor"),
        P("dp", "tensor"),
        P("tensor", "dp"),
    )
    return jax.shard_map(
        per_device, mesh=mesh, in_specs=in_specs, out_specs=out_specs, check_vma=False
    )
```

profile of v0, /device:TPU:0, one launch (start us, length us, event | category | flops | bytes accessed | tf_op | source)
XLA Modules:
  0.0 3971.7 jit_solution(5733695194731297895)
XLA Ops:
  15.3 14.4 all_gather.40
  29.8 14.7 all_gather.43
  44.6 15.8 all_gather.44
  60.4 14.7 all_gather.45
  75.1 49.1 %all-gather.10.cloned.1.call-done = bf16[4096,1024]{1,0:T(8,128)(2,1)} async-done(((bf16[1024,1024]{1,0:T(8,128)(2,1)}), bf16[4096,1024]{1,0:T(8,128)(2,1)}) %all-gather.10.cloned.1.call-update) | async-done | bytes 8388624 | tf_op jit(solution)/shard_map/all_gather | solution.py:174
  124.2 15.1 fusion.99
  166.4 15.1 multiply_reduce_fusion.4
  185.7 12.3 multiply_bitcast_fusion
  231.3 15.0 fusion.98
  265.2 21.4 fusion.218
  296.1 1259.2 %custom-call.10 = f32[32,2,2,1,128,128]{4,5,3,2,1,0:T(8,128)} custom-call(f32[32,2,2,1,128,128]{5,4,3,2,1,0:T(8,128)} %add_bitcast_fusion), custom_call_target="InvertDiagBlocksLowerTriangular" | custom-call | tf_op jit(solution)/shard_map/jvp(jit(_solve_triangular))/vmap(vmap(vmap()))/triangular_solve | solution.py:77
  1565.6 23.1 fusion.75
  1588.7 11.6 fusion.215
  1616.0 19.6 fusion.153
  1646.7 263.2 %while.48 = (s32[]{:T(128)}, f32[2,2,128,128]{3,2,1,0:T(8,128)S(1)}, f32[32,2,2,64,128]{4,3,2,1,0:T(8,128)}, f32[32,2,2,128,128]{4,3,2,1,0:T(8,128)}, f32[32,2,2...) while((s32[]{:T(128)}, ...), condition=%wide.region_5.6_spmd.clone, body=%wide.region_4.5_spmd.clone.sunk | while | flops 302481408 | bytes 4070101 | solution.py:111
  1951.8 153.5 %reduce-scatter.24.cloned.1.call-done = f32[1024,1024]{1,0:T(8,128)} async-done(((f32[4096,1024]{1,0:T(8,128)}), f32[1024,1024]{1,0:T(8,128)}) %reduce-scatter.24.cloned.1.call-update) | async-done | bytes 4194320 | tf_op jit(solution)/shard_map/reduce_scatter | solution.py:196
  2115.3 18.0 all-gather.18.cloned.1.call-done
  2133.3 88.6 %all-gather.16.cloned.1.call-done = bf16[4096,1024]{1,0:T(8,128)(2,1)} async-done(((bf16[1024,1024]{1,0:T(8,128)(2,1)}), bf16[4096,1024]{1,0:T(8,128)(2,1)}) %all-gather.16.cloned.1.call-update) | async-done | bytes 8388624 | tf_op jit(solution)/shard_map/all_gather | solution.py:206
  2222.0 12.7 fusion.220
  2234.6 15.5 all-gather.20.cloned.1.call-done
  2250.1 12.4 fusion.221
  2262.5 14.4 all-gather.22.cloned.1.call-done
  2277.0 88.8 %all-gather.24.cloned.1.call-done = bf16[4096,1024]{1,0:T(8,128)(2,1)} async-done(((bf16[1024,1024]{1,0:T(8,128)(2,1)}), bf16[4096,1024]{1,0:T(8,128)(2,1)}) %all-gather.24.cloned.1.call-update) | async-done | bytes 8388624 | tf_op jit(solution)/shard_map/all_gather | solution.py:219
  2365.8 22.4 multiply_convert_fusion
  2388.2 13.6 fusion.222
  2401.8 13.7 convolution_add_fusion.5
  2416.8 11.7 convolution_convert_fusion
  2428.6 140.9 %reduce-scatter.28.cloned.1.call-done = f32[1024,1024]{1,0:T(8,128)} async-done(((f32[4096,1024]{1,0:T(8,128)}), f32[1024,1024]{1,0:T(8,128)}) %reduce-scatter.28.cloned.1.call-update) | async-done | bytes 4194320 | tf_op jit(solution)/shard_map/reduce_scatter | solution.py:228
  2574.6 84.4 %reduce-scatter.26.cloned.1.call-done = bf16[1024,1024]{1,0:T(8,128)(2,1)} async-done(((bf16[4096,1024]{1,0:T(8,128)(2,1)}), bf16[1024,1024]{1,0:T(8,128)(2,1)}) %reduce-scatter.26.cloned.1.call-update) | async-done | bytes 2097168 | tf_op jit(solution)/shard_map/reduce_scatter | solution.py:214
  2698.1 12.3 mul.791
  2733.9 20.0 all-gather.26.cloned.1.call-done
  2753.9 13.3 fusion.119
  2804.5 588.0 %while.49 = (s32[]{:T(128)}, f32[2,2,128,128]{3,2,1,0:T(8,128)S(1)}, f32[32,2,2,128,128]{4,3,2,1,0:T(8,128)}, f32[32,2,2,128,128]{4,3,2,1,0:T(8,128)}, f32[32,2,...) while((s32[]{:T(128)}, ...), condition=%wide.region_16.17_spmd.clone, body=%wide.region_14.16_spmd.clone.sunk | while | flops 604766208 | bytes 6826808 | solution.py:111
  3392.5 23.8 fusion.80
  3416.3 21.4 fusion.79
  3437.7 22.1 fusion.93
  3459.8 17.1 fusion.103
  3476.9 19.7 fusion.105
  3496.6 17.3 multiply_reduce_fusion.1
  3520.5 12.4 add_bitcast_fusion.1
  3558.1 24.3 add_add_fusion.1
  3588.3 14.1 multiply_reduce_fusion.3
  3659.7 11.5 reshape.415
  3687.1 14.6 broadcast_in_dim.170
  3732.0 13.7 fusion.84
  3799.6 25.5 add_convert_fusion
  3841.1 76.0 %reduce-scatter.30.cloned.1.call-done = bf16[1024,1024]{1,0:T(8,128)(2,1)} async-done(((bf16[4096,1024]{1,0:T(8,128)(2,1)}), bf16[1024,1024]{1,0:T(8,128)(2,1)}) %reduce-scatter.30.cloned.1.call-update) | async-done | bytes 2097168 | tf_op jit(solution)/shard_map/reduce_scatter | solution.py:247
  3920.3 39.6 all-reduce.7
  (1067 shorter events, 1362.8 us)
Async XLA Ops:
  7.2 67.9 %all-gather.12.cloned.1.call-start = ((), (), s32[]{:S(2)}) async-start(), calls=%async_computation.14 | async-start | bytes 1179648 | tf_op jit(solution)/shard_map/all_gather | solution.py:166
  8.0 36.6 copy-start.88
  8.0 116.2 %all-gather.10.cloned.1.call-start = ((), (), s32[]{:S(2)}) async-start(), calls=%async_computation.13 | async-start | bytes 10485760 | tf_op jit(solution)/shard_map/all_gather | solution.py:174
  10.1 50.2 %copy-start.89 = (bf16[256,128]{1,0:T(8,128)(2,1)S(1)}, bf16[256,128]{1,0:T(8,128)(2,1)}, u32[]{:S(2)}) copy-start(bf16[256,128]{1,0:T(8,128)(2,1)} %param.34) | copy-start | bytes 196612
  13.6 217.7 %all-gather.14.cloned.1.call-start = ((), (), s32[]{:S(2)}) async-start(), calls=%async_computation.15 | async-start | bytes 1179648 | tf_op jit(solution)/shard_map/all_gather | solution.py:167
  14.4 2090.9 %reduce-scatter.24.cloned.1.call-start = ((), (), s32[]{:S(2)}) async-start(), calls=%async_computation.16 | async-start | bytes 20971520 | tf_op jit(solution)/shard_map/reduce_scatter | solution.py:196
  15.2 182.9 %copy-start.98 = (f32[2]{0:T(128)}, f32[2]{0:T(128)S(1)}, u32[]{:S(2)}) copy-start(f32[2]{0:T(128)S(1)} %fusion.204) | copy-start | bytes 28
  15.3 182.8 %copy-start.101 = (f32[2]{0:T(128)}, f32[2]{0:T(128)S(1)}, u32[]{:S(2)}) copy-start(f32[2]{0:T(128)S(1)} %dynamic_slice.110) | copy-start | bytes 28
  29.6 131.0 %copy-start.85 = (bf16[1024,6]{0,1:T(8,128)(2,1)}, bf16[1024,6]{0,1:T(8,128)(2,1)S(1)}, u32[]{:S(2)}) copy-start(bf16[1024,6]{0,1:T(8,128)(2,1)S(1)} %all_gather.40) | copy-start | bytes 36868
  29.7 256.9 %copy-start.79 = (pred[128,128]{1,0:T(8,128)(4,1)}, pred[128,128]{1,0:T(8,128)(4,1)S(1)}, u32[]{:S(2)}) copy-start(pred[128,128]{1,0:T(8,128)(4,1)S(1)} %get-tuple-element.891) | copy-start | bytes 49156
  29.8 256.9 %copy-start.81 = (pred[128,128]{1,0:T(8,128)(4,1)}, pred[128,128]{1,0:T(8,128)(4,1)S(1)}, u32[]{:S(2)}) copy-start(pred[128,128]{1,0:T(8,128)(4,1)S(1)} %get-tuple-element.892) | copy-start | bytes 49156
  44.5 157.4 %copy-start.44 = (bf16[1024,256]{1,0:T(8,128)(2,1)}, bf16[1024,256]{1,0:T(8,128)(2,1)S(1)}, u32[]{:S(2)}) copy-start(bf16[1024,256]{1,0:T(8,128)(2,1)S(1)} %all_gather.43) | copy-start | bytes 1572868
  44.6 1571.4 %copy-start.83 = (pred[64,128]{1,0:T(8,128)(4,1)}, pred[64,128]{1,0:T(8,128)(4,1)S(1)}, u32[]{:S(2)}) copy-start(pred[64,128]{1,0:T(8,128)(4,1)S(1)} %iota_compare_fusion.4) | copy-start | bytes 24580
  166.4 31.7 copy-start.70
  200.4 30.7 copy-start.40
  201.8 1414.2 %copy-start.30 = (f32[32,2,2,128]{3,2,1,0:T(2,128)}, f32[32,2,2,128]{3,2,1,0:T(2,128)S(1)}, u32[]{:S(2)}) copy-start(f32[32,2,2,128]{3,2,1,0:T(2,128)S(1)} %copy.437) | copy-start | bytes 196612
  201.9 1414.1 %copy-start.28 = (f32[32,2,2,128]{3,2,1,0:T(2,128)}, f32[32,2,2,128]{3,2,1,0:T(2,128)S(1)}, u32[]{:S(2)}) copy-start(f32[32,2,2,128]{3,2,1,0:T(2,128)S(1)} %copy.435) | copy-start | bytes 196612
  222.7 1386.3 %copy-start.50 = (f32[32,2,2,128]{0,3,2,1:T(8,128)}, f32[32,2,2,128]{0,3,2,1:T(8,128)S(1)}, u32[]{:S(2)}) copy-start(f32[32,2,2,128]{0,3,2,1:T(8,128)S(1)} %copy.441) | copy-start | bytes 196612
  231.2 1324.1 %copy-start.56 = (f32[32,2,2,128]{3,2,1,0:T(2,128)}, f32[32,2,2,128]{3,2,1,0:T(2,128)S(1)}, u32[]{:S(2)}) copy-start(f32[32,2,2,128]{3,2,1,0:T(2,128)S(1)} %copy.439) | copy-start | bytes 196612
  231.3 1324.1 %copy-start.58 = (f32[32,2,2,128]{3,2,1,0:T(2,128)}, f32[32,2,2,128]{3,2,1,0:T(2,128)S(1)}, u32[]{:S(2)}) copy-start(f32[32,2,2,128]{3,2,1,0:T(2,128)S(1)} %copy.433) | copy-start | bytes 196612
  1951.2 154.1 %copy-start.7 = (bf16[1024,1024]{1,0:T(8,128)(2,1)S(1)}, bf16[1024,1024]{1,0:T(8,128)(2,1)}, u32[]{:S(2)}) copy-start(bf16[1024,1024]{1,0:T(8,128)(2,1)} %param.21) | copy-start | bytes 6291460
  1951.2 182.1 %all-gather.18.cloned.1.call-start = ((), (), s32[]{:S(2)}) async-start(), calls=%async_computation.18 | async-start | bytes 1622016 | tf_op jit(solution)/shard_map/all_gather | solution.py:201
  1951.8 158.3 %copy-start.93 = (f32[1024]{0:T(1024)S(1)}, f32[1024]{0:T(1024)}, u32[]{:S(2)}) copy-start(f32[1024]{0:T(1024)} %param.25) | copy-start | bytes 12292
  1951.8 270.2 %all-gather.16.cloned.1.call-start = ((), (), s32[]{:S(2)}) async-start(), calls=%async_computation.17 | async-start | bytes 10485760 | tf_op jit(solution)/shard_map/all_gather | solution.py:206
  2111.8 138.3 %all-gather.20.cloned.1.call-start = ((), (), s32[]{:S(2)}) async-start(), calls=%async_computation.19 | async-start | bytes 1622016 | tf_op jit(solution)/shard_map/all_gather | solution.py:202
  2112.6 164.4 %all-gather.22.cloned.1.call-start = ((), (), s32[]{:S(2)}) async-start(), calls=%async_computation.20 | async-start | bytes 1622016 | tf_op jit(solution)/shard_map/all_gather | solution.py:203
  2113.3 252.4 %all-gather.24.cloned.1.call-start = ((), (), s32[]{:S(2)}) async-start(), calls=%async_computation.22 | async-start | bytes 10485760 | tf_op jit(solution)/shard_map/all_gather | solution.py:219
  2115.3 454.2 %reduce-scatter.28.cloned.1.call-start = ((), (), s32[]{:S(2)}) async-start(), calls=%async_computation.23 | async-start | bytes 20971520 | tf_op jit(solution)/shard_map/reduce_scatter | solution.py:228
  2262.5 125.7 %copy-start.111 = (bf16[1024,704]{0,1:T(8,128)(2,1)S(1)}, bf16[1024,704]{0,1:T(8,128)(2,1)}, u32[]{:S(2)}) copy-start(bf16[1024,704]{0,1:T(8,128)(2,1)} %all-gather.18.cloned.1.call-done) | copy-start | bytes 4325380
  2415.5 243.5 %reduce-scatter.26.cloned.1.call-start = ((), (), s32[]{:S(2)}) async-start(), calls=%async_computation.21 | async-start | bytes 10485760 | tf_op jit(solution)/shard_map/reduce_scatter | solution.py:214
  2428.6 325.4 %all-gather.26.cloned.1.call-start = ((), (), s32[]{:S(2)}) async-start(), calls=%async_computation.24 | async-start | bytes 10485760 | tf_op jit(solution)/shard_map/all_gather | solution.py:237
  2666.2 1159.0 %reduce-scatter.44.cloned.1.call-start = ((), (), s32[]{:S(2)}) async-start(), calls=%async_computation.32 | async-start | bytes 1769472
  2678.1 1149.1 %reduce-scatter.46.cloned.1.call-start = ((), (), s32[]{:S(2)}) async-start(), calls=%async_computation.33 | async-start | bytes 1769472
  2690.0 1139.1 %reduce-scatter.48.cloned.1.call-start = ((), (), s32[]{:S(2)}) async-start(), calls=%async_computation.34 | async-start | bytes 1769472
  2733.7 1098.0 %reduce-scatter.40.cloned.1.call-start = ((), (), s32[]{:S(2)}) async-start(), calls=%async_computation.30 | async-start | bytes 294912
  3551.9 36.3 slice-start.2
  3558.1 30.1 slice-start.3
  3615.8 217.4 %reduce-scatter.42.cloned.1.call-start = ((), (), s32[]{:S(2)}) async-start(), calls=%async_computation.31 | async-start | bytes 589824
  3630.7 204.1 %reduce-scatter.32.cloned.1.call-start = ((), (), s32[]{:S(2)}) async-start(), calls=%async_computation.26 | async-start | bytes 589824 | tf_op jit(solution)/shard_map/reduce_scatter | solution.py:260
  3677.8 158.5 %reduce-scatter.38.cloned.1.call-start = ((), (), s32[]{:S(2)}) async-start(), calls=%async_computation.29 | async-start | bytes 589824 | tf_op jit(solution)/shard_map/reduce_scatter | solution.py:272
  3731.9 105.9 %reduce-scatter.34.cloned.1.call-start = ((), (), s32[]{:S(2)}) async-start(), calls=%async_computation.27 | async-start | bytes 1179648 | tf_op jit(solution)/shard_map/reduce_scatter | solution.py:263
  3755.7 83.7 %reduce-scatter.36.cloned.1.call-start = ((), (), s32[]{:S(2)}) async-start(), calls=%async_computation.28 | async-start | bytes 1179648 | tf_op jit(solution)/shard_map/reduce_scatter | solution.py:266
  3780.6 136.4 %reduce-scatter.30.cloned.1.call-start = ((), (), s32[]{:S(2)}) async-start(), calls=%async_computation.25 | async-start | bytes 10485760 | tf_op jit(solution)/shard_map/reduce_scatter | solution.py:247
  3825.1 91.9 %copy-start.8 = (bf16[1024,1024]{1,0:T(8,128)(2,1)S(1)}, bf16[1024,1024]{1,0:T(8,128)(2,1)}, u32[]{:S(2)}) copy-start(bf16[1024,1024]{1,0:T(8,128)(2,1)} %param.21) | copy-start | bytes 6291460
  3825.1 91.9 %copy-start.91 = (f32[1024]{0:T(1024)S(1)}, f32[1024]{0:T(1024)}, u32[]{:S(2)}) copy-start(f32[1024]{0:T(1024)} %copy-done.90) | copy-start | bytes 12292
  3825.2 91.9 %copy-start.94 = (f32[1024]{0:T(1024)S(1)}, f32[1024]{0:T(1024)}, u32[]{:S(2)}) copy-start(f32[1024]{0:T(1024)} %param.24) | copy-start | bytes 12292
  3826.4 93.9 %copy-start.97 = (f32[1024]{0:T(1024)S(1)}, f32[1024]{0:T(1024)}, u32[]{:S(2)}) copy-start(f32[1024]{0:T(1024)} %get-tuple-element.772) | copy-start | bytes 12292
  3826.4 93.9 %copy-start.106 = (f32[128]{0:T(128)S(1)}, f32[128]{0:T(128)}, u32[]{:S(2)}) copy-start(f32[128]{0:T(128)} %get-tuple-element.770) | copy-start | bytes 1540
  (100 other events, 894.7 us)
Sparse Core Ops, SparseCore 0:
  9.6 24.8 all-gather.11
  36.9 87.2 all-gather.9
  125.8 22.0 all-gather.13
  1951.3 153.9 reduce-scatter.23
  2106.7 26.5 all-gather.17
  2135.6 86.3 all-gather.15
  2223.5 26.5 all-gather.19
  2251.7 25.2 all-gather.21
  2279.4 86.3 all-gather.23
  2415.6 153.8 reduce-scatter.27
  2572.6 86.4 reduce-scatter.25
  2666.3 87.5 all-gather.25
  2756.3 34.2 reduce-scatter.43
  2792.9 32.2 reduce-scatter.45
  2827.5 31.9 reduce-scatter.47
  3615.9 30.4 reduce-scatter.39
  3648.4 29.0 reduce-scatter.41
  3679.7 29.1 reduce-scatter.31
  3732.0 30.9 reduce-scatter.37
  3765.3 30.5 reduce-scatter.33
  3798.3 30.6 reduce-scatter.35
  3832.3 84.6 reduce-scatter.29
where the time goes:
time: 3990 us; the launch traced here: 3970 us
  other arithmetic  1550 us (39%)
  matrix products  1230 us (31%)
  waiting for transfers between devices  753 us (19%)
  local copies, waits for them, and re-layouts  322 us (8%)
  blocking collectives  99.2 us (2%)
    another operation x3, other arithmetic, stretch_mixer(): jax.scipy.linalg.solve_triangular(lower, jnp.concatenate([value_rows, gro...  1270 us
    dot_general x96, matrix products, advance(): jnp.einsum('bhcp,bhpv->bhcv', score, delta, precision=HIGH)  207 us
    dot_general x96, matrix products, advance(): jnp.einsum('bhpk,bhkv->bhpv', mix_k, carried, precision=HIGH)  192 us
    dot_general x96, matrix products, advance(): jnp.einsum('bhpk,bhpv->bhkv', key_o, delta, precision=HIGH)  168 us
    dot_general x96, matrix products, advance(): jnp.einsum('bhck,bhkv->bhcv', query_d, carried, precision=HIGH)  163 us
    reduce_scatter x1, waiting for transfers between devices, per_device(): lax.psum_scatter(project(mixed_low, full_out), 'tensor', scatter_dimensio...  153 us
    reduce_scatter x1, waiting for transfers between devices, per_device(): lax.psum_scatter(times_trans(gate_grad_pre, full_gate) + times_trans(up_g...  141 us
    dot_general x9, matrix products, times_trans(): lax.dot_general(left, right, (((1,), (1,)), ((), ())), preferred_element_...  124 us
  transfers between devices with their start and end apart: 22, of which 11 were waited for; matrix products, arithmetic and copies ran while one was open for 33% of the time, Pallas kernels for 0%

commit v1 on v0

--- a/solution.py
+++ b/solution.py
@@ -216,7 +216,22 @@
     ).astype(jnp.float32)
     block_out = ((middle + mlp_sum) * mask).astype(jnp.bfloat16)
     grad_top = out_grad.astype(jnp.float32) * mask
-    grad_all = lax.all_gather(grad_top.astype(jnp.bfloat16), "tensor", axis=0, tiled=True)
+    x = grad_top.astype(jnp.bfloat16)
+    ways, here, step = (lax.axis_size("tensor"), lax.axis_index("tensor"), x.shape[0])
+    lengths_2 = [n * ways if d == 0 else n for d, n in enumerate(x.shape)]
+    full = lax.dynamic_update_slice_in_dim(jnp.zeros(lengths_2, x.dtype), x, here * step, axis=0)
+    going_up = going_down = x
+    for far in range(1, ways // 2 + 1):
+        going_up = lax.ppermute(going_up, "tensor", [(d, (d + 1) % ways) for d in range(ways)])
+        full = lax.dynamic_update_slice_in_dim(full, going_up, (here - far) % ways * step, axis=0)
+        if 2 * far < ways:
+            going_down = lax.ppermute(
+                going_down, "tensor", [(d, (d - 1) % ways) for d in range(ways)]
+            )
+            full = lax.dynamic_update_slice_in_dim(
+                full, going_down, (here + far) % ways * step, axis=0
+            )
+    grad_all = full
     hidden_grad = times_trans(grad_all, full_down)
     down_grad = trans_times(hidden, grad_all)
     up_grad_pre = (hidden_grad * gate_act).astype(jnp.bfloat16)

time: 3990 us -> 3980 us (level)
    ppermute x0 -> x3, waiting for transfers between devices: none -> 195 us  [the longest x2 117 us: per_device(): lax.ppermute(going_up, 'tensor', [(d, (d + 1) % ways) for d in range(ways)])]
    all_gather x1 -> x0, waiting for transfers between devices: 88.8 us -> none  [per_device(): lax.all_gather(grad_top.astype(jnp.bfloat16), 'tensor', axis=0, tiled=True)]
    all_gather x1, waiting for transfers between devices: 88.6 us -> 0.01 us  [per_device(): lax.all_gather((normed_two * ln2_gain).astype(jnp.bfloat16), 'tensor', ax...]
  transfers between devices with their start and end apart: 22 -> 24, of which waited for: 11 -> 9; matrix products, arithmetic and copies ran while one was open for 33% -> 33% of each run, Pallas kernels for 0% -> 0%
where the time goes in v1:
time: 3980 us; the launch traced here: 3960 us
  other arithmetic  1550 us (39%)
  matrix products  1230 us (31%)
  waiting for transfers between devices  721 us (18%)
  local copies, waits for them, and re-layouts  335 us (8%)
  blocking collectives  99.2 us (2%)
    another operation x3, other arithmetic, stretch_mixer(): jax.scipy.linalg.solve_triangular(lower, jnp.concatenate([value_rows, gro...  1270 us
    dot_general x96, matrix products, advance(): jnp.einsum('bhcp,bhpv->bhcv', score, delta, precision=HIGH)  208 us
    dot_general x96, matrix products, advance(): jnp.einsum('bhpk,bhkv->bhpv', mix_k, carried, precision=HIGH)  192 us
    dot_general x96, matrix products, advance(): jnp.einsum('bhpk,bhpv->bhkv', key_o, delta, precision=HIGH)  168 us
    dot_general x96, matrix products, advance(): jnp.einsum('bhck,bhkv->bhcv', query_d, carried, precision=HIGH)  163 us
    reduce_scatter x1, waiting for transfers between devices, per_device(): lax.psum_scatter(project(mixed_low, full_out), 'tensor', scatter_dimensio...  153 us
    reduce_scatter x1, waiting for transfers between devices, per_device(): lax.psum_scatter(times_trans(gate_grad_pre, full_gate) + times_trans(up_g...  141 us
    dot_general x9, matrix products, times_trans(): lax.dot_general(left, right, (((1,), (1,)), ((), ())), preferred_element_...  124 us
  transfers between devices with their start and end apart: 24, of which 9 were waited for; matrix products, arithmetic and copies ran while one was open for 33% of the time, Pallas kernels for 0%

profile of v1, /device:TPU:0, one launch (start us, length us, event | category | flops | bytes accessed | tf_op | source)
XLA Modules:
  0.0 3959.9 jit_solution(15148040263612115241)
XLA Ops:
  15.3 14.4 all_gather.37
  29.8 14.7 all_gather.40
  44.6 15.8 all_gather.41
  60.4 14.7 all_gather.42
  75.1 49.1 %all-gather.9.cloned.1.call-done = bf16[4096,1024]{1,0:T(8,128)(2,1)} async-done(((bf16[1024,1024]{1,0:T(8,128)(2,1)}), bf16[4096,1024]{1,0:T(8,128)(2,1)}) %all-gather.9.cloned.1.call-update) | async-done | bytes 8388624 | tf_op jit(solution)/shard_map/all_gather | solution.py:174
  124.2 15.1 fusion.99
  166.4 15.1 multiply_reduce_fusion.4
  185.7 12.3 multiply_bitcast_fusion
  231.4 15.0 fusion.98
  265.3 21.4 fusion.219
  296.4 1259.2 %custom-call.10 = f32[32,2,2,1,128,128]{4,5,3,2,1,0:T(8,128)} custom-call(f32[32,2,2,1,128,128]{5,4,3,2,1,0:T(8,128)} %add_bitcast_fusion), custom_call_target="InvertDiagBlocksLowerTriangular" | custom-call | tf_op jit(solution)/shard_map/jvp(jit(_solve_triangular))/vmap(vmap(vmap()))/triangular_solve | solution.py:77
  1565.9 23.1 fusion.75
  1589.0 11.6 fusion.216
  1616.6 19.6 fusion.153
  1647.3 263.2 %while.48 = (s32[]{:T(128)}, f32[2,2,128,128]{3,2,1,0:T(8,128)S(1)}, f32[32,2,2,64,128]{4,3,2,1,0:T(8,128)}, f32[32,2,2,128,128]{4,3,2,1,0:T(8,128)}, f32[32,2,2...) while((s32[]{:T(128)}, ...), condition=%wide.region_5.6_spmd.clone, body=%wide.region_4.5_spmd.clone.sunk | while | flops 302481408 | bytes 4070101 | solution.py:111
  1952.4 153.5 %reduce-scatter.24.cloned.1.call-done = f32[1024,1024]{1,0:T(8,128)} async-done(((f32[4096,1024]{1,0:T(8,128)}), f32[1024,1024]{1,0:T(8,128)}) %reduce-scatter.24.cloned.1.call-update) | async-done | bytes 4194320 | tf_op jit(solution)/shard_map/reduce_scatter | solution.py:196
  2122.5 68.2 %collective-permute-done = bf16[1024,1024]{1,0:T(8,128)(2,1)} collective-permute-done((bf16[1024,1024]{1,0:T(8,128)(2,1)}, bf16[1024,1024]{1,0:T(8,128)(2,1)}, u32[]{:S(2)}, u32[]{:S(2)}) %collective-permute-start) | collective-permute-done | bytes 2097184 | tf_op jit(solution)/shard_map/ppermute | solution.py:225
  2195.4 78.1 %collective-permute-done.1 = bf16[1024,1024]{1,0:T(8,128)(2,1)} collective-permute-done((bf16[1024,1024]{1,0:T(8,128)(2,1)}, bf16[1024,1024]{1,0:T(8,128)(2,1)}, u32[]{:S(2)}, u32[]{:S(2)}) %collective-permute-start.1) | collective-permute-done | bytes 2097184 | tf_op jit(solution)/shard_map/ppermute | solution.py:228
  2276.6 48.7 %collective-permute-done.2 = bf16[1024,1024]{1,0:T(8,128)(2,1)} collective-permute-done((bf16[1024,1024]{1,0:T(8,128)(2,1)}, bf16[1024,1024]{1,0:T(8,128)(2,1)}, u32[]{:S(2)}, u32[]{:S(2)}) %collective-permute-start.2) | collective-permute-done | bytes 2097184 | tf_op jit(solution)/shard_map/ppermute | solution.py:225
  2328.5 12.7 fusion.221
  2341.2 12.6 fusion.222
  2353.8 22.6 multiply_convert_fusion
  2376.4 13.6 fusion.223
  2390.0 13.6 convolution_add_fusion.5
  2405.0 11.7 convolution_convert_fusion
  2416.7 140.8 %reduce-scatter.28.cloned.1.call-done = f32[1024,1024]{1,0:T(8,128)} async-done(((f32[4096,1024]{1,0:T(8,128)}), f32[1024,1024]{1,0:T(8,128)}) %reduce-scatter.28.cloned.1.call-update) | async-done | bytes 4194320 | tf_op jit(solution)/shard_map/reduce_scatter | solution.py:243
  2562.7 84.2 %reduce-scatter.26.cloned.1.call-done = bf16[1024,1024]{1,0:T(8,128)(2,1)} async-done(((bf16[4096,1024]{1,0:T(8,128)(2,1)}), bf16[1024,1024]{1,0:T(8,128)(2,1)}) %reduce-scatter.26.cloned.1.call-update) | async-done | bytes 2097168 | tf_op jit(solution)/shard_map/reduce_scatter | solution.py:214
  2686.0 12.3 mul.804
  2721.8 20.0 all-gather.23.cloned.1.call-done
  2741.8 13.3 fusion.119
  2792.4 588.6 %while.49 = (s32[]{:T(128)}, f32[2,2,128,128]{3,2,1,0:T(8,128)S(1)}, f32[32,2,2,128,128]{4,3,2,1,0:T(8,128)}, f32[32,2,2,128,128]{4,3,2,1,0:T(8,128)}, f32[32,2,...) while((s32[]{:T(128)}, ...), condition=%wide.region_16.17_spmd.clone, body=%wide.region_14.16_spmd.clone.sunk | while | flops 604766208 | bytes 6826808 | solution.py:111
  3381.0 23.8 fusion.80
  3404.8 21.4 fusion.79
  3426.2 22.1 fusion.93
  3448.3 17.1 fusion.103
  3465.4 19.7 fusion.105
  3485.1 17.3 multiply_reduce_fusion.1
  3508.9 12.4 add_bitcast_fusion.1
  3546.6 24.3 add_add_fusion.1
  3576.7 14.1 multiply_reduce_fusion.3
  3648.1 11.5 reshape.415
  3675.4 14.6 broadcast_in_dim.174
  3690.0 11.5 broadcast_in_dim.175
  3701.6 11.5 reshape.412
  3720.3 13.6 fusion.84
  3788.0 25.5 add_convert_fusion
  3829.4 75.8 %reduce-scatter.30.cloned.1.call-done = bf16[1024,1024]{1,0:T(8,128)(2,1)} async-done(((bf16[4096,1024]{1,0:T(8,128)(2,1)}), bf16[1024,1024]{1,0:T(8,128)(2,1)}) %reduce-scatter.30.cloned.1.call-update) | async-done | bytes 2097168 | tf_op jit(solution)/shard_map/reduce_scatter | solution.py:262
  3908.5 39.6 all-reduce.7
  (1074 shorter events, 1358.9 us)
Async XLA Ops:
  7.2 67.9 %all-gather.11.cloned.1.call-start = ((), (), s32[]{:S(2)}) async-start(), calls=%async_computation.14 | async-start | bytes 1179648 | tf_op jit(solution)/shard_map/all_gather | solution.py:166
  8.0 36.6 copy-start.88
  8.0 116.2 %all-gather.9.cloned.1.call-start = ((), (), s32[]{:S(2)}) async-start(), calls=%async_computation.13 | async-start | bytes 10485760 | tf_op jit(solution)/shard_map/all_gather | solution.py:174
  10.1 50.3 %copy-start.89 = (bf16[256,128]{1,0:T(8,128)(2,1)S(1)}, bf16[256,128]{1,0:T(8,128)(2,1)}, u32[]{:S(2)}) copy-start(bf16[256,128]{1,0:T(8,128)(2,1)} %param.34) | copy-start | bytes 196612
  13.6 217.8 %all-gather.13.cloned.1.call-start = ((), (), s32[]{:S(2)}) async-start(), calls=%async_computation.15 | async-start | bytes 1179648 | tf_op jit(solution)/shard_map/all_gather | solution.py:167
  14.4 2091.5 %reduce-scatter.24.cloned.1.call-start = ((), (), s32[]{:S(2)}) async-start(), calls=%async_computation.16 | async-start | bytes 20971520 | tf_op jit(solution)/shard_map/reduce_scatter | solution.py:196
  15.2 182.9 %copy-start.98 = (f32[2]{0:T(128)}, f32[2]{0:T(128)S(1)}, u32[]{:S(2)}) copy-start(f32[2]{0:T(128)S(1)} %fusion.204) | copy-start | bytes 28
  15.3 182.8 %copy-start.101 = (f32[2]{0:T(128)}, f32[2]{0:T(128)S(1)}, u32[]{:S(2)}) copy-start(f32[2]{0:T(128)S(1)} %dynamic_slice.110) | copy-start | bytes 28
  29.7 130.9 %copy-start.85 = (bf16[1024,6]{0,1:T(8,128)(2,1)}, bf16[1024,6]{0,1:T(8,128)(2,1)S(1)}, u32[]{:S(2)}) copy-start(bf16[1024,6]{0,1:T(8,128)(2,1)S(1)} %all_gather.37) | copy-start | bytes 36868
  29.8 257.0 %copy-start.79 = (pred[128,128]{1,0:T(8,128)(4,1)}, pred[128,128]{1,0:T(8,128)(4,1)S(1)}, u32[]{:S(2)}) copy-start(pred[128,128]{1,0:T(8,128)(4,1)S(1)} %get-tuple-element.893) | copy-start | bytes 49156
  29.8 257.0 %copy-start.81 = (pred[128,128]{1,0:T(8,128)(4,1)}, pred[128,128]{1,0:T(8,128)(4,1)S(1)}, u32[]{:S(2)}) copy-start(pred[128,128]{1,0:T(8,128)(4,1)S(1)} %get-tuple-element.894) | copy-start | bytes 49156
  44.5 157.4 %copy-start.44 = (bf16[1024,256]{1,0:T(8,128)(2,1)}, bf16[1024,256]{1,0:T(8,128)(2,1)S(1)}, u32[]{:S(2)}) copy-start(bf16[1024,256]{1,0:T(8,128)(2,1)S(1)} %all_gather.40) | copy-start | bytes 1572868
  44.6 1572.0 %copy-start.83 = (pred[64,128]{1,0:T(8,128)(4,1)}, pred[64,128]{1,0:T(8,128)(4,1)S(1)}, u32[]{:S(2)}) copy-start(pred[64,128]{1,0:T(8,128)(4,1)S(1)} %iota_compare_fusion.4) | copy-start | bytes 24580
  166.4 31.7 copy-start.70
  200.4 30.7 copy-start.40
  201.8 1414.8 %copy-start.30 = (f32[32,2,2,128]{3,2,1,0:T(2,128)}, f32[32,2,2,128]{3,2,1,0:T(2,128)S(1)}, u32[]{:S(2)}) copy-start(f32[32,2,2,128]{3,2,1,0:T(2,128)S(1)} %copy.437) | copy-start | bytes 196612
  201.9 1414.7 %copy-start.28 = (f32[32,2,2,128]{3,2,1,0:T(2,128)}, f32[32,2,2,128]{3,2,1,0:T(2,128)S(1)}, u32[]{:S(2)}) copy-start(f32[32,2,2,128]{3,2,1,0:T(2,128)S(1)} %copy.435) | copy-start | bytes 196612
  222.7 1386.5 %copy-start.50 = (f32[32,2,2,128]{0,3,2,1:T(8,128)}, f32[32,2,2,128]{0,3,2,1:T(8,128)S(1)}, u32[]{:S(2)}) copy-start(f32[32,2,2,128]{0,3,2,1:T(8,128)S(1)} %copy.441) | copy-start | bytes 196612
  231.3 1324.4 %copy-start.56 = (f32[32,2,2,128]{3,2,1,0:T(2,128)}, f32[32,2,2,128]{3,2,1,0:T(2,128)S(1)}, u32[]{:S(2)}) copy-start(f32[32,2,2,128]{3,2,1,0:T(2,128)S(1)} %copy.439) | copy-start | bytes 196612
  231.4 1324.3 %copy-start.58 = (f32[32,2,2,128]{3,2,1,0:T(2,128)}, f32[32,2,2,128]{3,2,1,0:T(2,128)S(1)}, u32[]{:S(2)}) copy-start(f32[32,2,2,128]{3,2,1,0:T(2,128)S(1)} %copy.433) | copy-start | bytes 196612
  1951.7 154.2 %copy-start.7 = (bf16[1024,1024]{1,0:T(8,128)(2,1)S(1)}, bf16[1024,1024]{1,0:T(8,128)(2,1)}, u32[]{:S(2)}) copy-start(bf16[1024,1024]{1,0:T(8,128)(2,1)} %param.21) | copy-start | bytes 6291460
  1951.7 376.8 %all-gather.17.cloned.1.call-start = ((), (), s32[]{:S(2)}) async-start(), calls=%async_computation.18 | async-start | bytes 1622016 | tf_op jit(solution)/shard_map/all_gather | solution.py:201
  1952.3 158.5 %copy-start.93 = (f32[1024]{0:T(1024)S(1)}, f32[1024]{0:T(1024)}, u32[]{:S(2)}) copy-start(f32[1024]{0:T(1024)} %param.25) | copy-start | bytes 12292
  1952.3 376.2 %all-gather.15.cloned.1.call-start = ((), (), s32[]{:S(2)}) async-start(), calls=%async_computation.17 | async-start | bytes 10485760 | tf_op jit(solution)/shard_map/all_gather | solution.py:206
  2112.5 228.7 %all-gather.19.cloned.1.call-start = ((), (), s32[]{:S(2)}) async-start(), calls=%async_computation.19 | async-start | bytes 1622016 | tf_op jit(solution)/shard_map/all_gather | solution.py:202
  2119.5 71.2 %collective-permute-start = (bf16[1024,1024]{1,0:T(8,128)(2,1)}, bf16[1024,1024]{1,0:T(8,128)(2,1)}, u32[]{:S(2)}, u32[]{:S(2)}) collective-permute-start(bf16[1024,1024]{1,0:T(8,128)(2,1)} %get-tuple-element.852), channel_id=1, source_target_pairs={{0,1},{1,2},{2,3},{3,0},{4,5},{5,6},{6,7},{7,4},{8,9},{9,10},{10,1... | collective-permute-start | bytes 6291464 | tf_op jit(solution)/shard_map/ppermute | solution.py:225
  2120.9 232.9 %all-gather.21.cloned.1.call-start = ((), (), s32[]{:S(2)}) async-start(), calls=%async_computation.20 | async-start | bytes 1622016 | tf_op jit(solution)/shard_map/all_gather | solution.py:203
  2120.9 152.6 %collective-permute-start.1 = (bf16[1024,1024]{1,0:T(8,128)(2,1)}, bf16[1024,1024]{1,0:T(8,128)(2,1)}, u32[]{:S(2)}, u32[]{:S(2)}) collective-permute-start(bf16[1024,1024]{1,0:T(8,128)(2,1)} %get-tuple-element.852), channel_id=1, source_target_pairs={{0,3},{1,0},{2,1},{3,2},{4,7},{5,4},{6,5},{7,6},{8,11},{9,8},{10,9... | collective-permute-start | bytes 6291464 | tf_op jit(solution)/shard_map/ppermute | solution.py:228
  2190.7 134.6 %collective-permute-start.2 = (bf16[1024,1024]{1,0:T(8,128)(2,1)}, bf16[1024,1024]{1,0:T(8,128)(2,1)}, u32[]{:S(2)}, u32[]{:S(2)}) collective-permute-start(bf16[1024,1024]{1,0:T(8,128)(2,1)} %collective-permute-done), channel_id=1, source_target_pairs={{0,1},{1,2},{2,3},{3,0},{4,5},{5,6},{6,7},{7,4},{8,9},{9,10},{10,1... | collective-permute-start | bytes 6291464 | tf_op jit(solution)/shard_map/ppermute | solution.py:225
  2192.2 365.4 %reduce-scatter.28.cloned.1.call-start = ((), (), s32[]{:S(2)}) async-start(), calls=%async_computation.22 | async-start | bytes 20971520 | tf_op jit(solution)/shard_map/reduce_scatter | solution.py:243
  2403.6 243.2 %reduce-scatter.26.cloned.1.call-start = ((), (), s32[]{:S(2)}) async-start(), calls=%async_computation.21 | async-start | bytes 10485760 | tf_op jit(solution)/shard_map/reduce_scatter | solution.py:214
  2416.7 325.1 %all-gather.23.cloned.1.call-start = ((), (), s32[]{:S(2)}) async-start(), calls=%async_computation.23 | async-start | bytes 10485760 | tf_op jit(solution)/shard_map/all_gather | solution.py:252
  2654.1 1159.5 %reduce-scatter.44.cloned.1.call-start = ((), (), s32[]{:S(2)}) async-start(), calls=%async_computation.31 | async-start | bytes 1769472
  2665.9 1149.6 %reduce-scatter.46.cloned.1.call-start = ((), (), s32[]{:S(2)}) async-start(), calls=%async_computation.32 | async-start | bytes 1769472
  2677.9 1139.6 %reduce-scatter.48.cloned.1.call-start = ((), (), s32[]{:S(2)}) async-start(), calls=%async_computation.33 | async-start | bytes 1769472
  2721.6 1098.5 %reduce-scatter.40.cloned.1.call-start = ((), (), s32[]{:S(2)}) async-start(), calls=%async_computation.29 | async-start | bytes 294912
  3540.4 36.3 slice-start.2
  3604.2 217.3 %reduce-scatter.42.cloned.1.call-start = ((), (), s32[]{:S(2)}) async-start(), calls=%async_computation.30 | async-start | bytes 589824
  3619.1 204.0 %reduce-scatter.32.cloned.1.call-start = ((), (), s32[]{:S(2)}) async-start(), calls=%async_computation.25 | async-start | bytes 589824 | tf_op jit(solution)/shard_map/reduce_scatter | solution.py:275
  3666.2 158.4 %reduce-scatter.38.cloned.1.call-start = ((), (), s32[]{:S(2)}) async-start(), calls=%async_computation.28 | async-start | bytes 589824 | tf_op jit(solution)/shard_map/reduce_scatter | solution.py:287
  3720.3 105.9 %reduce-scatter.34.cloned.1.call-start = ((), (), s32[]{:S(2)}) async-start(), calls=%async_computation.26 | async-start | bytes 1179648 | tf_op jit(solution)/shard_map/reduce_scatter | solution.py:278
  3744.1 83.7 %reduce-scatter.36.cloned.1.call-start = ((), (), s32[]{:S(2)}) async-start(), calls=%async_computation.27 | async-start | bytes 1179648 | tf_op jit(solution)/shard_map/reduce_scatter | solution.py:281
  3769.0 136.2 %reduce-scatter.30.cloned.1.call-start = ((), (), s32[]{:S(2)}) async-start(), calls=%async_computation.24 | async-start | bytes 10485760 | tf_op jit(solution)/shard_map/reduce_scatter | solution.py:262
  3813.5 91.7 %copy-start.8 = (bf16[1024,1024]{1,0:T(8,128)(2,1)S(1)}, bf16[1024,1024]{1,0:T(8,128)(2,1)}, u32[]{:S(2)}) copy-start(bf16[1024,1024]{1,0:T(8,128)(2,1)} %param.21) | copy-start | bytes 6291460
  3813.5 91.7 %copy-start.91 = (f32[1024]{0:T(1024)S(1)}, f32[1024]{0:T(1024)}, u32[]{:S(2)}) copy-start(f32[1024]{0:T(1024)} %copy-done.90) | copy-start | bytes 12292
  3813.5 91.7 %copy-start.94 = (f32[1024]{0:T(1024)S(1)}, f32[1024]{0:T(1024)}, u32[]{:S(2)}) copy-start(f32[1024]{0:T(1024)} %param.24) | copy-start | bytes 12292
  3814.8 93.7 %copy-start.97 = (f32[1024]{0:T(1024)S(1)}, f32[1024]{0:T(1024)}, u32[]{:S(2)}) copy-start(f32[1024]{0:T(1024)} %get-tuple-element.772) | copy-start | bytes 12292
  3814.8 93.7 %copy-start.106 = (f32[128]{0:T(128)S(1)}, f32[128]{0:T(128)}, u32[]{:S(2)}) copy-start(f32[128]{0:T(128)} %get-tuple-element.770) | copy-start | bytes 1540
  (102 other events, 948.5 us)
Sparse Core Ops, SparseCore 0:
  9.6 24.8 all-gather.10
  36.9 87.2 all-gather.8
  125.8 22.0 all-gather.12
  1951.8 153.9 reduce-scatter.23
  2107.3 26.5 all-gather.16
  2136.1 153.4 all-gather.14
  2291.3 26.5 all-gather.18
  2319.4 25.2 all-gather.20
  2403.8 153.7 reduce-scatter.27
  2560.5 86.3 reduce-scatter.25
  2654.2 87.6 all-gather.22
  2744.1 34.2 reduce-scatter.43
  2780.8 32.3 reduce-scatter.45
  2815.5 32.1 reduce-scatter.47
  3604.3 30.2 reduce-scatter.39
  3636.8 29.1 reduce-scatter.41
  3668.2 29.0 reduce-scatter.31
  3720.4 30.9 reduce-scatter.37
  3753.7 30.5 reduce-scatter.33
  3786.5 30.5 reduce-scatter.35
  3820.4 84.7 reduce-scatter.29
